TPU v7x, 128 devices: a whole 4x4x4 slice. The times are simulated.
128 devices in a mesh: row: 8 (over z, core), col: 16 (over y, x).
Axes of the slice: x: 4, y: 4, z: 4, core: 2. Of those that a mesh axis runs over, the one named last changes fastest.
Arguments:
- front_entries: float32 [16384, 16384], P(None, ('row', 'col')), as said below
- child_updates: float32 [4096, 128, 128], P(('row', 'col')), may hold values from -1 to 1
- row_maps: int32 [4096, 128], P(('row', 'col')), may hold values from 0 to 127, each once within a row
- col_maps: int32 [4096, 128], P(('row', 'col')), may hold values from 0 to 127, each once within a row
- target_columns: int32 [4096, 1], P(('row', 'col')), may hold values from 0 to 127; in each aligned block of 32 rows (0 to 31, 32 to 63, ...) at most 2 rows name the same one
- row_offsets: int32 [4096, 1], P(('row', 'col')), may hold values from 0 to 127
Outputs:
- factored: float32 [16, 8, 8, 16, 128, 128], P(None, 'row', None, 'col')
Inputs may be any that keep to these rules, and one draw needn't show every extreme that they name: `target_columns`: within the rows of one device (aligned blocks of 32 rows) no block column is named more than 2 times; some device names one block column exactly 2 times. `row_maps`: each row is a permutation of 0 to 127. `col_maps`: each row is a permutation of 0 to 127. `front_entries`: entries off the diagonal lie in [0, 2]; diagonal entries lie between 2.5 and 3.5 times the square root of 16384.
All inputs are finite; a program needn't handle non-finite values.
Results may differ from a plain program's by a relative error of at most 0.0001.
Values sent between devices are 32-bit elements; how exact they have to be, the bound alone decides.
A program may use at most 192 MiB of HBM per device.

v0:
```python
import jax
import jax.numpy as jnp
from jax import lax
from jax.sharding import PartitionSpec as P

SLOTS = 2
PANELS = 2
PRECISE = lax.Precision.HIGHEST


def broadcast(value, axis, source):
    kept = jnp.where(lax.axis_index(axis) == source, value, 0).astype(value.dtype)
    return lax.psum(kept, axis)


def place_tiles(tile_set, row_set, col_set):
    levels = jnp.arange(tile_set.shape[1], dtype=jnp.int32)
    row_onehot = (row_set[:, :, None] == levels).astype(jnp.float32)
    col_onehot = (col_set[:, :, None] == levels).astype(jnp.float32)
    half_done = jnp.einsum("nij,njb->nib", tile_set, col_onehot, precision=PRECISE)
    return jnp.einsum("nia,nib->nab", row_onehot, half_done, precision=PRECISE)


def local(front_entries, child_updates, row_maps, col_maps, target_columns, row_offsets):
    grid_rows = lax.axis_size("row")
    grid_cols = lax.axis_size("col")
    block_count = grid_rows * grid_cols
    tile_edge = child_updates.shape[1]
    held_count = child_updates.shape[0]
    columns = target_columns[:, 0]
    offsets = row_offsets[:, 0]
    target_rows = columns + offsets % (block_count - columns)
    placed = place_tiles(child_updates, row_maps, col_maps)
    serial = jnp.arange(held_count, dtype=jnp.int32)
    earlier = (columns[:, None] == columns[None, :]) & (serial[None, :] < serial[:, None])
    slot_rank = jnp.sum(earlier.astype(jnp.int32), axis=1)
    position = columns * SLOTS + slot_rank
    outgoing = (
        jnp.zeros((block_count * SLOTS, tile_edge, tile_edge), jnp.float32).at[position].set(placed)
    )
    targets = jnp.zeros((block_count * SLOTS,), jnp.int32).at[position].set(target_rows)
    arrived, landing = (
        lax.all_to_all(outgoing, ("row", "col"), split_axis=0, concat_axis=0, tiled=True),
        lax.all_to_all(targets, ("row", "col"), split_axis=0, concat_axis=0, tiled=True),
    )
    own_blocks = front_entries.reshape(block_count, tile_edge, tile_edge)
    column_blocks = own_blocks + jax.ops.segment_sum(arrived, landing, num_segments=block_count)
    grid_tiles = lax.all_to_all(
        column_blocks.reshape(block_count // grid_rows, grid_rows, tile_edge, tile_edge),
        "row",
        split_axis=1,
        concat_axis=1,
        tiled=True,
    )
    my_row = lax.axis_index("row")
    my_col = lax.axis_index("col")
    block_rows = jnp.arange(block_count // grid_rows, dtype=jnp.int32) * grid_rows + my_row
    block_cols = jnp.arange(block_count // grid_cols, dtype=jnp.int32) * grid_cols + my_col
    stride = grid_cols // grid_rows
    for panel_idx in range(PANELS):
        local_row = panel_idx // grid_rows
        prepare_local_col = panel_idx // grid_cols
        pivot_tile = broadcast(
            grid_tiles[local_row, prepare_local_col], "row", panel_idx % grid_rows
        )
        symmetric = jnp.tril(pivot_tile) + jnp.tril(pivot_tile, -1).T
        pivot_factor = jnp.linalg.cholesky(symmetric)
        panel_rows = grid_tiles[:, prepare_local_col].reshape(-1, tile_edge)
        solved = jax.scipy.linalg.solve_triangular(pivot_factor, panel_rows.T, lower=True).T
        solved = solved.reshape(-1, tile_edge, tile_edge)
        lower_part = jnp.where((block_rows > panel_idx)[:, None, None], solved, 0.0)
        prepare_written = jnp.where(
            (block_rows == panel_idx)[:, None, None], pivot_factor[None], lower_part
        )
        prepare_shared = broadcast(lower_part, "col", panel_idx % grid_cols)
        chosen = lax.dynamic_index_in_dim(
            prepare_shared.reshape(block_count // grid_cols, stride, tile_edge, tile_edge),
            my_col // grid_rows,
            1,
            keepdims=False,
        )
        prepare_across = broadcast(chosen, "row", my_col % grid_rows)
        tiles_now = grid_tiles - jnp.einsum(
            "jab,scb->jsac", prepare_shared, prepare_across, precision=PRECISE
        )
        local_col = panel_idx // grid_cols
        fresh = jnp.where(my_col == panel_idx % grid_cols, prepare_written, tiles_now[:, local_col])
        grid_tiles = tiles_now.at[:, local_col].set(fresh)
    row_grid = block_rows[:, None, None, None]
    col_grid = block_cols[None, :, None, None]
    inside = jnp.arange(tile_edge)[:, None] >= jnp.arange(tile_edge)[None, :]
    keep_mask = (row_grid > col_grid) | (row_grid == col_grid) & inside[None, None]
    result = jnp.where(keep_mask, grid_tiles, 0.0)
    return result.reshape(
        block_count // grid_rows, 1, block_count // grid_cols, 1, tile_edge, tile_edge
    )


def solution(mesh):
    return jax.shard_map(
        local,
        mesh=mesh,
        in_specs=(
            P(None, ("row", "col")),
            P(("row", "col"), None, None),
            P(("row", "col"), None),
            P(("row", "col"), None),
            P(("row", "col"), None),
            P(("row", "col"), None),
        ),
        out_specs=P(None, "row", None, "col", None, None),
        check_vma=False,
    )
```

profile of v0, /device:TPU:0, one launch (start us, length us, event | category | flops | bytes accessed | tf_op | source)
XLA Modules:
  0.0 978.0 jit_solution(2281378333469623732)
XLA Ops:
  6.5 6.0 copy.132
  12.6 0.2 convert_reduce_fusion
  12.8 0.1 fusion.28
  12.9 0.7 scatter_custom_fusion
  13.6 0.8 all_to_all.12
  14.3 11.2 %all-to-all-start = ((s32[128,2,1]{1,2,0:T(1,128)}), s32[128,2,1]{1,2,0:T(1,128)S(1)}, u32[]{:S(2)}, u32[]{:S(2)}) async-start(s32[128,2,1]{1,2,0:T(1,128)} %bitcast.5), calls=%async_computation | async-start | bytes 131072 | tf_op jit(solution)/shard_map/all_to_all | solution.py:44
  25.5 2.3 fusion.1
  27.8 2.3 fusion
  30.1 7.8 broadcast_in_dim.130
  37.9 5.5 scatter_fusion
  43.4 10.3 %all-to-all-start.1 = ((f32[256,128,128]{2,1,0:T(8,128)}), f32[256,128,128]{2,1,0:T(8,128)}, u32[]{:S(2)}, u32[]{:S(2)}) async-start(f32[256,128,128]{2,1,0:T(8,128)} %scatter_fusion), calls=%async_computation.1 | async-start | bytes 33554432 | tf_op jit(solution)/shard_map/all_to_all | solution.py:43
  53.7 0.6 broadcast.303
  54.2 0.8 reduce.11
  55.1 0.1 reshape.269
  55.2 218.6 %all-to-all-done.1 = f32[256,128,128]{2,1,0:T(8,128)} async-done(((f32[256,128,128]{2,1,0:T(8,128)}), f32[256,128,128]{2,1,0:T(8,128)}, u32[]{:S(2)}, u32[]{:S(2)}) %all-to-all-start.1) | async-done | bytes 16777248 | tf_op jit(solution)/shard_map/all_to_all | solution.py:43
  273.8 55.1 %scatter_fusion.1 = f32[128,128,128]{2,1,0:T(8,128)} fusion(f32[128,128,128]{2,1,0:T(8,128)} %bitcast.110, s32[256]{0:T(256)S(1)} %reshape.269, f32[256,128,128]{2,1,0:T(8,128)} %all-to-all-done.1), kind=kCustom, calls=%fused_computation.2 | custom fusion | flops 4194304 | bytes 50332672 | tf_op jit(solution)/shard_map/scatter-add | solution.py:47
  328.9 7.7 copy.86
  336.6 32.8 %all-to-all-start.2 = ((f32[16,8,128,128]{3,2,0,1:T(8,128)}), f32[16,8,128,128]{3,2,0,1:T(8,128)}, u32[]{:S(2)}, u32[]{:S(2)}) async-start(f32[16,8,128,128]{3,2,0,1:T(8,128)} %copy.86), calls=%async_computation.2 | async-start | bytes 16777216 | tf_op jit(solution)/shard_map/all_to_all | solution.py:48
  369.4 94.6 %all-to-all-done.2 = f32[16,8,128,128]{3,2,0,1:T(8,128)} async-done(((f32[16,8,128,128]{3,2,0,1:T(8,128)}), f32[16,8,128,128]{3,2,0,1:T(8,128)}, u32[]{:S(2)}, u32[]{:S(2)}) %all-to-all-start.2) | async-done | bytes 8388640 | tf_op jit(solution)/shard_map/all_to_all | solution.py:48
  464.1 1.5 fusion.21
  465.6 0.2 all-reduce.9.cloned.1.call-start
  465.8 1.3 slice.81
  467.1 59.4 %all-reduce.7.cloned.1.call-done = f32[128,128]{1,0:T(8,128)} async-done(((f32[128,128]{1,0:T(8,128)}), f32[128,128]{1,0:T(8,128)}) %all-reduce.7.cloned.1.call-update) | async-done | bytes 65552 | tf_op jit(solution)/shard_map/psum | solution.py:13
  526.6 0.9 copy.88
  527.5 0.9 bitcast_add_fusion.3
  528.4 0.1 copy.90
  528.5 11.7 %cholesky.44 = f32[128,128]{1,0:T(8,128)S(1)} custom-call(f32[128,128]{1,0:T(8,128)S(1)} %fusion.25), custom_call_target="Cholesky" | custom-call | tf_op jit(solution)/shard_map/jit(cholesky)/cholesky | solution.py:67
  540.3 0.6 compare_reduce_fusion.1
  540.9 0.7 select_bitcast_fusion.2
  541.6 9.8 %custom-call.6 = f32[1,128,128]{1,2,0:T(8,128)S(1)} custom-call(f32[1,128,128]{2,1,0:T(8,128)S(1)} %get-tuple-element.33), custom_call_target="InvertDiagBlocksLowerTriangular" | custom-call | tf_op jit(solution)/shard_map/jit(_solve_triangular)/triangular_solve | solution.py:69
  551.4 1.1 convolution_bitcast_fusion.1
  552.5 0.3 copy.108
  552.8 1.1 select_select_fusion.2
  554.1 86.0 %all-reduce.9.cloned.1.call-done = f32[16,128,128]{2,1,0:T(8,128)} async-done(((f32[16,128,128]{2,1,0:T(8,128)}), f32[16,128,128]{2,1,0:T(8,128)}) %all-reduce.9.cloned.1.call-update) | async-done | bytes 1048592 | tf_op jit(solution)/shard_map/psum | solution.py:13
  640.1 1.9 fusion.13
  642.2 60.8 %all-reduce.11.cloned.1.call-done = f32[8,128,128]{2,1,0:T(8,128)} async-done(((f32[8,128,128]{2,1,0:T(8,128)}), f32[8,128,128]{2,1,0:T(8,128)}) %all-reduce.11.cloned.1.call-update) | async-done | bytes 524304 | tf_op jit(solution)/shard_map/psum | solution.py:13
  703.0 10.0 %bitcast_subtract_fusion.1 = f32[16,8,128,128]{3,2,1,0:T(8,128)S(1)} fusion(f32[16,128,128]{2,1,0:T(8,128)} %all-reduce.9.cloned.1.call-done, f32[8,128,128]{2,1,0:T(8,128)} %all-reduce.11.cloned.1.call-done, f32[16,8,128,128]{3,2,0,1:T(8,128)} %all-to-all-done.2), kind=kOutput, calls=%fused_computation.4 | convolution fusion | flops 3223322624 | bytes 18350080 | tf_op jit(solution)/shard_map/jab,scb->jsac/dot_general | solution.py:83
  713.0 3.4 copy-done.2
  716.4 1.2 fusion.34
  717.6 0.6 fusion.20
  718.3 0.3 all-reduce.15.cloned.1.call-start
  718.6 0.1 copy.84
  718.7 0.1 copy.98
  718.8 1.6 copy.99
  720.4 57.2 %all-reduce.13.cloned.1.call-done = f32[128,128]{1,0:T(8,128)} async-done(((f32[128,128]{1,0:T(8,128)}), f32[128,128]{1,0:T(8,128)}) %all-reduce.13.cloned.1.call-update) | async-done | bytes 65552 | tf_op jit(solution)/shard_map/psum | solution.py:13
  777.5 0.8 broadcast_select_fusion
  778.4 0.1 copy.96
  778.5 0.9 bitcast_add_fusion.1
  779.4 0.1 copy.97
  779.5 11.7 %cholesky.55 = f32[128,128]{1,0:T(8,128)S(1)} custom-call(f32[128,128]{1,0:T(8,128)S(1)} %fusion.23), custom_call_target="Cholesky" | custom-call | tf_op jit(solution)/shard_map/jit(cholesky)/cholesky | solution.py:67
  791.3 0.7 compare_reduce_fusion
  792.0 0.7 select_bitcast_fusion.1
  792.7 9.8 %custom-call.7 = f32[1,128,128]{1,2,0:T(8,128)S(1)} custom-call(f32[1,128,128]{2,1,0:T(8,128)S(1)} %get-tuple-element.31), custom_call_target="InvertDiagBlocksLowerTriangular" | custom-call | tf_op jit(solution)/shard_map/jit(_solve_triangular)/triangular_solve | solution.py:69
  802.6 2.4 convolution_bitcast_fusion
  804.9 1.6 copy.100
  806.5 1.2 select_select_fusion
  807.7 0.3 all-reduce.17.cloned.1.call-start
  808.1 85.7 %all-reduce.15.cloned.1.call-done = f32[16,128,128]{2,1,0:T(8,128)} async-done(((f32[16,128,128]{2,1,0:T(8,128)}), f32[16,128,128]{2,1,0:T(8,128)}) %all-reduce.15.cloned.1.call-update) | async-done | bytes 1048592 | tf_op jit(solution)/shard_map/psum | solution.py:13
  893.8 1.9 fusion.12
  895.8 1.0 constant_dynamic-update-slice_fusion
  896.8 59.7 %all-reduce.17.cloned.1.call-done = f32[8,128,128]{2,1,0:T(8,128)} async-done(((f32[8,128,128]{2,1,0:T(8,128)}), f32[8,128,128]{2,1,0:T(8,128)}) %all-reduce.17.cloned.1.call-update) | async-done | bytes 524304 | tf_op jit(solution)/shard_map/psum | solution.py:13
  956.5 10.1 %bitcast_subtract_fusion = f32[16,8,128,128]{3,2,1,0:T(8,128)S(1)} fusion(f32[16,8,128,128]{3,2,1,0:T(8,128)} %constant_dynamic-update-slice_fusion, f32[16,128,128]{2,1,0:T(8,128)} %all-reduce.15.cloned.1.call-done, f32[8,128,128]{2,1,0:T(8,128)} %all-reduce.17.cloned.1.call-done), kind=kOutput, calls=%fused_computation.3 | convolution fusion | flops 3223322624 | bytes 18350080 | tf_op jit(solution)/shard_map/jab,scb->jsac/dot_general | solution.py:83
  966.6 0.3 fusion.6
  966.9 4.2 select_bitcast_fusion
  (39 shorter events, 0.6 us)
Async XLA Ops:
  6.5 19.0 %copy-start = (f32[32,128,128]{2,1,0:T(8,128)S(1)}, f32[32,128,128]{2,1,0:T(8,128)}, u32[]{:S(2)}) copy-start(f32[32,128,128]{2,1,0:T(8,128)} %param.14) | copy-start | bytes 6291460
  6.5 6.0 copy-start.5
  6.5 6.2 copy-start.6
  6.5 19.0 %copy-start.3 = (s32[32,128]{1,0:T(8,128)S(1)}, s32[32,128]{1,0:T(8,128)}, u32[]{:S(2)}) copy-start(s32[32,128]{1,0:T(8,128)} %param.16) | copy-start | bytes 49156
  6.5 21.3 %copy-start.4 = (s32[32,128]{1,0:T(8,128)S(1)}, s32[32,128]{1,0:T(8,128)}, u32[]{:S(2)}) copy-start(s32[32,128]{1,0:T(8,128)} %param.15) | copy-start | bytes 49156
  14.3 29.1 %all-to-all-start = ((s32[128,2,1]{1,2,0:T(1,128)}), s32[128,2,1]{1,2,0:T(1,128)S(1)}, u32[]{:S(2)}, u32[]{:S(2)}) async-start(s32[128,2,1]{1,2,0:T(1,128)} %bitcast.5), calls=%async_computation | async-start | bytes 131072 | tf_op jit(solution)/shard_map/all_to_all | solution.py:44
  43.4 230.4 %all-to-all-start.1 = ((f32[256,128,128]{2,1,0:T(8,128)}), f32[256,128,128]{2,1,0:T(8,128)}, u32[]{:S(2)}, u32[]{:S(2)}) async-start(f32[256,128,128]{2,1,0:T(8,128)} %scatter_fusion), calls=%async_computation.1 | async-start | bytes 33554432 | tf_op jit(solution)/shard_map/all_to_all | solution.py:43
  336.6 127.5 %all-to-all-start.2 = ((f32[16,8,128,128]{3,2,0,1:T(8,128)}), f32[16,8,128,128]{3,2,0,1:T(8,128)}, u32[]{:S(2)}, u32[]{:S(2)}) async-start(f32[16,8,128,128]{3,2,0,1:T(8,128)} %copy.86), calls=%async_computation.2 | async-start | bytes 16777216 | tf_op jit(solution)/shard_map/all_to_all | solution.py:48
  369.4 157.2 %all-reduce.7.cloned.1.call-start = ((), (), s32[]{:S(2)}) async-start(), calls=%async_computation.3 | async-start | bytes 131072 | tf_op jit(solution)/shard_map/psum | solution.py:13
  465.6 174.6 %all-reduce.9.cloned.1.call-start = ((), (), s32[]{:S(2)}) async-start(), calls=%async_computation.4 | async-start | bytes 2097152 | tf_op jit(solution)/shard_map/psum | solution.py:13
  554.0 149.0 %all-reduce.11.cloned.1.call-start = ((), (), s32[]{:S(2)}) async-start(), calls=%async_computation.5 | async-start | bytes 1048576 | tf_op jit(solution)/shard_map/psum | solution.py:13
  642.0 135.5 %all-reduce.13.cloned.1.call-start = ((), (), s32[]{:S(2)}) async-start(), calls=%async_computation.6 | async-start | bytes 131072 | tf_op jit(solution)/shard_map/psum | solution.py:13
  713.0 3.4 copy-start.2
  718.3 175.5 %all-reduce.15.cloned.1.call-start = ((), (), s32[]{:S(2)}) async-start(), calls=%async_computation.7 | async-start | bytes 2097152 | tf_op jit(solution)/shard_map/psum | solution.py:13
  807.7 148.8 %all-reduce.17.cloned.1.call-start = ((), (), s32[]{:S(2)}) async-start(), calls=%async_computation.8 | async-start | bytes 1048576 | tf_op jit(solution)/shard_map/psum | solution.py:13
  966.9 4.3 copy-start.1
Sparse Core Ops, SparseCore 0:
  465.7 60.8 all-reduce.6
  554.1 85.9 all-reduce.8
  642.5 60.4 all-reduce.10
  718.4 59.0 all-reduce.12
  807.8 85.9 all-reduce.14
  896.0 60.4 all-reduce.16
where the time goes:
time: 979 us; the launch traced here: 978 us
  waiting for transfers between devices  722 us (74%)
  other arithmetic  119 us (12%)
  starting transfers between devices  55.1 us (6%)
  local copies, waits for them, and re-layouts  39.9 us (4%)
  matrix products  28.1 us (3%)
  between operations  13.9 us (1%)
    psum x6, waiting for transfers between devices, broadcast(): return lax.psum(kept, axis)  409 us
    all_to_all x1, waiting for transfers between devices, local(): lax.all_to_all(outgoing, ('row', 'col'), split_axis=0, concat_axis=0, til...  219 us
    all_to_all x1, waiting for transfers between devices, local(): lax.all_to_all(column_blocks.reshape(block_count // grid_rows, grid_rows,...  94.6 us
    scatter-add x1, other arithmetic, local(): jax.ops.segment_sum(arrived, landing, num_segments=block_count)  55.1 us
    all_to_all x1, starting transfers between devices, local(): lax.all_to_all(column_blocks.reshape(block_count // grid_rows, grid_rows,...  32.8 us
    another operation x6, other arithmetic, local(): pivot_factor = jnp.linalg.cholesky(symmetric)  24.9 us
    another operation x4, other arithmetic, local(): jax.scipy.linalg.solve_triangular(pivot_factor, panel_rows.T, lower=True)  21 us
    dot_general x2, matrix products, local(): jnp.einsum('jab,scb->jsac', prepare_shared, prepare_across, precision=PRE...  20.1 us
  transfers between devices with their start and end apart: 9, of which 8 were waited for; matrix products, arithmetic and copies ran while one was open for 2% of the time, Pallas kernels for 0%

commit v1 on v0

--- a/solution.py
+++ b/solution.py
@@ -10,7 +10,7 @@
 
 def broadcast(value, axis, source):
     kept = jnp.where(lax.axis_index(axis) == source, value, 0).astype(value.dtype)
-    return lax.psum(kept, axis)
+    return jnp.sum(lax.all_gather(kept, axis), axis=0)
 
 
 def place_tiles(tile_set, row_set, col_set):

time: 979 us -> 917 us (0.937)
  waiting for transfers between devices: 722 us -> 598 us
  blocking collectives: 0 us -> 26.7 us
  local copies, waits for them, and re-layouts: 39.9 us -> 54.6 us
  other arithmetic: 119 us -> 132 us
    psum x6 -> x0, waiting for transfers between devices: 409 us -> none  [broadcast(): return lax.psum(kept, axis)]
    all_gather x0 -> x4, waiting for transfers between devices: none -> 284 us  [broadcast(): return jnp.sum(lax.all_gather(kept, axis), axis=0)]
    all_gather x0 -> x2, blocking collectives: none -> 26.7 us  [broadcast(): return jnp.sum(lax.all_gather(kept, axis), axis=0)]
    reduce_sum x0 -> x6, other arithmetic: none -> 20 us  [broadcast(): return jnp.sum(lax.all_gather(kept, axis), axis=0)]
  transfers between devices with their start and end apart: 9 -> 7, of which waited for: 8 -> 6; matrix products, arithmetic and copies ran while one was open for 2% -> 2% of each run, Pallas kernels for 0% -> 0%
where the time goes in v1:
time: 917 us; the launch traced here: 907 us
  waiting for transfers between devices  598 us (65%)
  other arithmetic  132 us (14%)
  starting transfers between devices  54.8 us (6%)
  local copies, waits for them, and re-layouts  54.6 us (6%)
  matrix products  27.6 us (3%)
  blocking collectives  26.7 us (3%)
  between operations  13.8 us (2%)
    all_gather x4, waiting for transfers between devices, broadcast(): return jnp.sum(lax.all_gather(kept, axis), axis=0)  284 us
    all_to_all x1, waiting for transfers between devices, local(): lax.all_to_all(outgoing, ('row', 'col'), split_axis=0, concat_axis=0, til...  219 us
    all_to_all x1, waiting for transfers between devices, local(): lax.all_to_all(column_blocks.reshape(block_count // grid_rows, grid_rows,...  94.6 us
    scatter-add x1, other arithmetic, local(): jax.ops.segment_sum(arrived, landing, num_segments=block_count)  55.1 us
    all_to_all x1, starting transfers between devices, local(): lax.all_to_all(column_blocks.reshape(block_count // grid_rows, grid_rows,...  32.8 us
    all_gather x2, blocking collectives, broadcast(): return jnp.sum(lax.all_gather(kept, axis), axis=0)  26.7 us
    another operation x6, other arithmetic, local(): pivot_factor = jnp.linalg.cholesky(symmetric)  24.9 us
    another operation x4, other arithmetic, local(): jax.scipy.linalg.solve_triangular(pivot_factor, panel_rows.T, lower=True)  21 us
  transfers between devices with their start and end apart: 7, of which 6 were waited for; matrix products, arithmetic and copies ran while one was open for 2% of the time, Pallas kernels for 0%

profile of v1, /device:TPU:0, one launch (start us, length us, event | category | flops | bytes accessed | tf_op | source)
XLA Modules:
  0.0 907.3 jit_solution(10450341239794513907)
XLA Ops:
  6.5 6.0 copy.99
  12.6 0.2 convert_reduce_fusion
  12.8 0.1 fusion.28
  12.9 0.7 scatter_custom_fusion
  13.6 0.8 all_to_all.12
  14.3 11.2 %all-to-all-start = ((s32[128,2,1]{1,2,0:T(1,128)}), s32[128,2,1]{1,2,0:T(1,128)S(1)}, u32[]{:S(2)}, u32[]{:S(2)}) async-start(s32[128,2,1]{1,2,0:T(1,128)} %bitcast.5), calls=%async_computation | async-start | bytes 131072 | tf_op jit(solution)/shard_map/all_to_all | solution.py:44
  25.5 2.3 fusion.1
  27.8 2.3 fusion
  30.1 7.8 broadcast_in_dim.130
  37.9 5.5 scatter_fusion
  43.4 10.3 %all-to-all-start.1 = ((f32[256,128,128]{2,1,0:T(8,128)}), f32[256,128,128]{2,1,0:T(8,128)}, u32[]{:S(2)}, u32[]{:S(2)}) async-start(f32[256,128,128]{2,1,0:T(8,128)} %scatter_fusion), calls=%async_computation.1 | async-start | bytes 33554432 | tf_op jit(solution)/shard_map/all_to_all | solution.py:43
  53.7 0.6 broadcast.419
  54.2 0.8 reduce.13
  55.1 0.1 reshape.335
  55.2 218.6 %all-to-all-done.1 = f32[256,128,128]{2,1,0:T(8,128)} async-done(((f32[256,128,128]{2,1,0:T(8,128)}), f32[256,128,128]{2,1,0:T(8,128)}, u32[]{:S(2)}, u32[]{:S(2)}) %all-to-all-start.1) | async-done | bytes 16777248 | tf_op jit(solution)/shard_map/all_to_all | solution.py:43
  273.8 55.1 %scatter_fusion.1 = f32[128,128,128]{2,1,0:T(8,128)} fusion(f32[128,128,128]{2,1,0:T(8,128)} %bitcast.108, s32[256]{0:T(256)S(1)} %reshape.335, f32[256,128,128]{2,1,0:T(8,128)} %all-to-all-done.1), kind=kCustom, calls=%fused_computation.2 | custom fusion | flops 4194304 | bytes 50332672 | tf_op jit(solution)/shard_map/scatter-add | solution.py:47
  328.9 7.7 copy.56
  336.6 32.8 %all-to-all-start.2 = ((f32[16,8,128,128]{3,2,0,1:T(8,128)}), f32[16,8,128,128]{3,2,0,1:T(8,128)}, u32[]{:S(2)}, u32[]{:S(2)}) async-start(f32[16,8,128,128]{3,2,0,1:T(8,128)} %copy.56), calls=%async_computation.2 | async-start | bytes 16777216 | tf_op jit(solution)/shard_map/all_to_all | solution.py:48
  369.5 94.6 %all-to-all-done.2 = f32[16,8,128,128]{3,2,0,1:T(8,128)} async-done(((f32[16,8,128,128]{3,2,0,1:T(8,128)}), f32[16,8,128,128]{3,2,0,1:T(8,128)}, u32[]{:S(2)}, u32[]{:S(2)}) %all-to-all-start.2) | async-done | bytes 8388640 | tf_op jit(solution)/shard_map/all_to_all | solution.py:48
  464.1 0.8 fusion.19
  464.9 13.6 %all-gather = f32[8,1,128,128]{3,2,1,0:T(8,128)S(1)} all-gather(f32[1,1,128,128]{3,2,1,0:T(8,128)S(1)} %fusion.19), channel_id=2, replica_groups=mesh['row'=8,'col'=16] {'row'}, dimensions={0}, use_global_device_ids=true | all-gather | bytes 589824 | tf_op jit(solution)/shard_map/all_gather | solution.py:13
  478.8 11.7 %cholesky.44 = f32[128,128]{1,0:T(8,128)S(1)} custom-call(f32[128,128]{1,0:T(8,128)S(1)} %fusion.24), custom_call_target="Cholesky" | custom-call | tf_op jit(solution)/shard_map/jit(cholesky)/cholesky | solution.py:67
  490.6 0.6 compare_reduce_fusion.1
  491.2 0.7 select_bitcast_fusion.2
  491.9 9.8 %custom-call.6 = f32[1,128,128]{1,2,0:T(8,128)S(1)} custom-call(f32[1,128,128]{2,1,0:T(8,128)S(1)} %get-tuple-element.33), custom_call_target="InvertDiagBlocksLowerTriangular" | custom-call | tf_op jit(solution)/shard_map/jit(_solve_triangular)/triangular_solve | solution.py:69
  501.7 1.3 slice.81
  503.0 1.1 convolution_bitcast_fusion.1
  504.1 0.3 copy.81
  504.4 1.1 select_select_fusion.2
  505.7 112.3 %all-gather.9.cloned.1.call-done = f32[16,16,128,128]{3,2,1,0:T(8,128)} async-done(((f32[1,16,128,128]{3,2,1,0:T(8,128)}), f32[16,16,128,128]{3,2,1,0:T(8,128)}) %all-gather.9.cloned.1.call-update) | async-done | bytes 16777232 | tf_op jit(solution)/shard_map/all_gather | solution.py:13
  618.0 7.4 reduce_sum.73
  625.4 1.4 copy.85
  626.8 2.5 constant_dynamic-slice_fusion.1
  629.3 1.9 copy.87
  631.2 1.9 broadcast_select_fusion.1
  633.1 0.2 all-gather.11.cloned.1.call-start
  633.5 31.2 %all-gather.13.cloned.1.call-done = f32[64,1,128,128]{3,2,1,0:T(8,128)} async-done(((f32[8,1,128,128]{3,2,1,0:T(8,128)}), f32[64,1,128,128]{3,2,1,0:T(8,128)}) %all-gather.13.cloned.1.call-update) | async-done | bytes 4194320 | tf_op jit(solution)/shard_map/all_gather | solution.py:13
  664.7 2.5 bitcast_reduce_fusion.1
  667.3 9.8 %bitcast_subtract_fusion.1 = f32[16,8,128,128]{3,2,0,1:T(8,128)S(1)} fusion(f32[16,8,128,128]{3,2,0,1:T(8,128)} %all-to-all-done.2, f32[16,128,128]{2,1,0:T(8,128)S(1)} %reduce_sum.73, f32[8,128,128]{2,1,0:T(8,128)S(1)} %bitcast_reduce_fusion.1), kind=kOutput, calls=%fused_computation.4 | convolution fusion | flops 3223322624 | bytes 18350080 | tf_op jit(solution)/shard_map/jab,scb->jsac/dot_general | solution.py:83
  677.1 3.4 copy-done.2
  680.5 1.2 fusion.34
  681.7 13.1 %all-gather.2 = f32[8,1,128,128]{3,2,1,0:T(8,128)S(1)} all-gather(f32[1,1,128,128]{3,2,1,0:T(8,128)S(1)} %fusion.18), channel_id=4, replica_groups=mesh['row'=8,'col'=16] {'row'}, dimensions={0}, use_global_device_ids=true | all-gather | bytes 589824 | tf_op jit(solution)/shard_map/all_gather | solution.py:13
  695.1 11.7 %cholesky.55 = f32[128,128]{1,0:T(8,128)S(1)} custom-call(f32[128,128]{1,0:T(8,128)S(1)} %fusion.21), custom_call_target="Cholesky" | custom-call | tf_op jit(solution)/shard_map/jit(cholesky)/cholesky | solution.py:67
  706.9 0.7 compare_reduce_fusion
  707.6 0.7 select_bitcast_fusion.1
  708.3 9.8 %custom-call.7 = f32[1,128,128]{1,2,0:T(8,128)S(1)} custom-call(f32[1,128,128]{2,1,0:T(8,128)S(1)} %get-tuple-element.31), custom_call_target="InvertDiagBlocksLowerTriangular" | custom-call | tf_op jit(solution)/shard_map/jit(_solve_triangular)/triangular_solve | solution.py:69
  718.1 1.6 copy.83
  719.8 2.4 convolution_bitcast_fusion
  722.1 1.5 copy.84
  723.7 1.2 select_select_fusion
  724.9 0.3 all-gather.15.cloned.1.call-start
  725.2 110.5 %all-gather.11.cloned.1.call-done = f32[16,16,128,128]{3,2,1,0:T(8,128)} async-done(((f32[1,16,128,128]{3,2,1,0:T(8,128)}), f32[16,16,128,128]{3,2,1,0:T(8,128)}) %all-gather.11.cloned.1.call-update) | async-done | bytes 16777232 | tf_op jit(solution)/shard_map/all_gather | solution.py:13
  835.7 7.5 reduce_sum.77
  843.2 1.4 copy.86
  844.6 2.5 constant_dynamic-slice_fusion
  847.1 1.9 copy.88
  849.0 1.9 broadcast_select_fusion
  851.2 1.0 constant_dynamic-update-slice_fusion
  852.2 30.3 %all-gather.15.cloned.1.call-done = f32[64,1,128,128]{3,2,1,0:T(8,128)} async-done(((f32[8,1,128,128]{3,2,1,0:T(8,128)}), f32[64,1,128,128]{3,2,1,0:T(8,128)}) %all-gather.15.cloned.1.call-update) | async-done | bytes 4194320 | tf_op jit(solution)/shard_map/all_gather | solution.py:13
  882.6 2.5 bitcast_reduce_fusion
  885.1 9.8 %bitcast_subtract_fusion = f32[16,8,128,128]{3,2,0,1:T(8,128)S(1)} fusion(f32[16,8,128,128]{3,2,0,1:T(8,128)} %constant_dynamic-update-slice_fusion, f32[16,128,128]{2,1,0:T(8,128)S(1)} %reduce_sum.77, f32[8,128,128]{2,1,0:T(8,128)S(1)} %bitcast_reduce_fusion), kind=kOutput, calls=%fused_computation.3 | convolution fusion | flops 3223322624 | bytes 18350080 | tf_op jit(solution)/shard_map/jab,scb->jsac/dot_general | solution.py:83
  894.9 0.3 fusion.6
  895.2 1.3 select_bitcast_fusion
  896.5 4.0 copy.77
  (51 shorter events, 1.4 us)
Async XLA Ops:
  6.5 19.0 %copy-start = (f32[32,128,128]{2,1,0:T(8,128)S(1)}, f32[32,128,128]{2,1,0:T(8,128)}, u32[]{:S(2)}) copy-start(f32[32,128,128]{2,1,0:T(8,128)} %param.14) | copy-start | bytes 6291460
  6.5 6.0 copy-start.7
  6.5 6.2 copy-start.8
  6.5 19.0 %copy-start.5 = (s32[32,128]{1,0:T(8,128)S(1)}, s32[32,128]{1,0:T(8,128)}, u32[]{:S(2)}) copy-start(s32[32,128]{1,0:T(8,128)} %param.16) | copy-start | bytes 49156
  6.5 21.3 %copy-start.6 = (s32[32,128]{1,0:T(8,128)S(1)}, s32[32,128]{1,0:T(8,128)}, u32[]{:S(2)}) copy-start(s32[32,128]{1,0:T(8,128)} %param.15) | copy-start | bytes 49156
  14.3 29.1 %all-to-all-start = ((s32[128,2,1]{1,2,0:T(1,128)}), s32[128,2,1]{1,2,0:T(1,128)S(1)}, u32[]{:S(2)}, u32[]{:S(2)}) async-start(s32[128,2,1]{1,2,0:T(1,128)} %bitcast.5), calls=%async_computation | async-start | bytes 131072 | tf_op jit(solution)/shard_map/all_to_all | solution.py:44
  43.4 230.4 %all-to-all-start.1 = ((f32[256,128,128]{2,1,0:T(8,128)}), f32[256,128,128]{2,1,0:T(8,128)}, u32[]{:S(2)}, u32[]{:S(2)}) async-start(f32[256,128,128]{2,1,0:T(8,128)} %scatter_fusion), calls=%async_computation.1 | async-start | bytes 33554432 | tf_op jit(solution)/shard_map/all_to_all | solution.py:43
  336.6 127.5 %all-to-all-start.2 = ((f32[16,8,128,128]{3,2,0,1:T(8,128)}), f32[16,8,128,128]{3,2,0,1:T(8,128)}, u32[]{:S(2)}, u32[]{:S(2)}) async-start(f32[16,8,128,128]{3,2,0,1:T(8,128)} %copy.56), calls=%async_computation.2 | async-start | bytes 16777216 | tf_op jit(solution)/shard_map/all_to_all | solution.py:48
  369.4 248.6 %all-gather.9.cloned.1.call-start = ((), (), s32[]{:S(2)}) async-start(), calls=%async_computation.3 | async-start | bytes 17825792 | tf_op jit(solution)/shard_map/all_gather | solution.py:13
  505.6 159.2 %all-gather.13.cloned.1.call-start = ((), (), s32[]{:S(2)}) async-start(), calls=%async_computation.5 | async-start | bytes 4718592 | tf_op jit(solution)/shard_map/all_gather | solution.py:13
  633.1 202.6 %all-gather.11.cloned.1.call-start = ((), (), s32[]{:S(2)}) async-start(), calls=%async_computation.4 | async-start | bytes 17825792 | tf_op jit(solution)/shard_map/all_gather | solution.py:13
  677.1 3.4 copy-start.2
  681.7 43.5 %copy-start.3 = (f32[16,1,128,128]{3,2,0,1:T(8,128)}, f32[16,1,128,128]{3,2,0,1:T(8,128)S(1)}, u32[]{:S(2)}) copy-start(f32[16,1,128,128]{3,2,0,1:T(8,128)S(1)} %get-tuple-element.36) | copy-start | bytes 3145732
  724.9 157.7 %all-gather.15.cloned.1.call-start = ((), (), s32[]{:S(2)}) async-start(), calls=%async_computation.6 | async-start | bytes 4718592 | tf_op jit(solution)/shard_map/all_gather | solution.py:13
  835.7 15.5 %copy-start.4 = (f32[16,1,128,128]{3,2,0,1:T(8,128)S(1)}, f32[16,1,128,128]{3,2,0,1:T(8,128)}, u32[]{:S(2)}) copy-start(f32[16,1,128,128]{3,2,0,1:T(8,128)} %copy-done.3) | copy-start | bytes 3145732
  895.2 5.3 copy-start.1
Sparse Core Ops, SparseCore 0:
  505.7 112.2 all-gather.8
  633.2 31.4 all-gather.12
  725.0 110.6 all-gather.10
  851.0 31.4 all-gather.14
